TPU v7x, 512 devices: a whole 4x8x8 slice. The times are simulated.
512 devices in a mesh: ta: 8 (over x, y_lo), ha: 8 (over y_hi, core), wa: 8 (over z).
Axes of the slice: x: 4, y: 8 (y_hi: 4, y_lo: 2; y = y_hi * 2 + y_lo), z: 8, core: 2. Of those that a mesh axis runs over, the one named last changes fastest.
Arguments:
- queries: bfloat16 [24, 32, 64, 1536], P('ta', 'ha', 'wa'), may hold values from -6 to 6
- keys: bfloat16 [24, 32, 64, 1536], P('ta', 'ha', 'wa'), may hold values from -6 to 6
- values: bfloat16 [24, 32, 64, 1536], P('ta', 'ha', 'wa'), may hold values from -6 to 6
- radius: int32 [12, 3], replicated, may hold values from 0 to 1
- out_weight: bfloat16 [1536, 3072], P(('ha', 'wa')), may hold values from -0.15625 to 0.15625
Outputs:
- mixed_out: bfloat16 [24, 32, 64, 3072], P('ta', 'ha', 'wa')
All inputs are finite; a program needn't handle non-finite values.
Results may differ from a plain program's by a relative error of at most 0.0057.
Values may be sent and summed in bfloat16 or wider, within the bound.
A program may use at most 128 MiB of HBM per device.

v0:
```python
import math

import jax
import jax.numpy as jnp
from jax import lax
from jax.sharding import PartitionSpec as P

D = 3072
TILE = 4


def padded(block, sides, width):
    for axis, dim in sides:
        count = lax.axis_size(axis)
        forward = [(i, i + 1) for i in range(count - 1)]
        backward = [(target, source) for source, target in forward]
        low = lax.ppermute(
            lax.slice_in_dim(block, block.shape[dim] - width, None, axis=dim), axis, forward
        )
        high = lax.ppermute(lax.slice_in_dim(block, 0, width, axis=dim), axis, backward)
        block = jnp.concatenate([low, block, high], axis=dim)
    return block


def shifted(value, axis, steps):
    count = lax.axis_size(axis)
    initial, last = (max(0, -steps), min(count, count - steps))
    return lax.ppermute(value, axis, [(source, source + steps) for source in range(initial, last)])


def allow_axis(base_index, count, margin, tile_len, total, reach):
    query_pos = base_index + jnp.arange(count, dtype=jnp.int32)
    key_pos = base_index - margin + jnp.arange(count + 2 * margin, dtype=jnp.int32)
    inside = (key_pos >= 0) & (key_pos < total)
    apart = jnp.abs(query_pos[:, None] // tile_len - key_pos[None, :] // tile_len)
    return (apart[None, :, :] <= reach[:, None, None]) & inside[None, None, :]


def shards(queries, keys, values, radius, out_weight):
    frame_count, row_count, column_count, features = queries.shape
    head_count = radius.shape[0]
    head_dim = features // head_count
    stacked = jnp.stack([keys, values])
    spread = padded(stacked, (("ha", 2), ("wa", 3)), TILE)
    earlier = shifted(spread[:, frame_count - 1 :], "ta", 1)
    later_frame = shifted(spread[:, :1], "ta", -1)
    window = jnp.concatenate([earlier, spread, later_frame], axis=1)
    allow_t = allow_axis(
        lax.axis_index("ta") * frame_count,
        frame_count,
        1,
        1,
        frame_count * lax.axis_size("ta"),
        radius[:, 0],
    )
    allow_h = allow_axis(
        lax.axis_index("ha") * row_count,
        row_count,
        TILE,
        TILE,
        row_count * lax.axis_size("ha"),
        radius[:, 1],
    )
    allow_w = allow_axis(
        lax.axis_index("wa") * column_count,
        column_count,
        TILE,
        TILE,
        column_count * lax.axis_size("wa"),
        radius[:, 2],
    )
    allowed = (
        allow_t[:, :, None, None, :, None, None]
        & allow_h[:, None, :, None, None, :, None]
        & allow_w[:, None, None, :, None, None, :]
    )
    query_count = frame_count * row_count * column_count
    allowed = allowed.reshape(head_count, query_count, -1)
    query_rows = queries.reshape(query_count, head_count, head_dim)
    key_rows = window[0].reshape(-1, head_count, head_dim)
    value_rows = window[1].reshape(-1, head_count, head_dim)
    scores = jnp.einsum(
        "qhd,khd->hqk", query_rows, key_rows, preferred_element_type=jnp.float32
    ) * (1.0 / math.sqrt(head_dim))
    scores = jnp.where(allowed, scores, -jnp.inf)
    biggest = jnp.max(scores, axis=-1, keepdims=True)
    expo = jnp.exp(scores - biggest)
    probs = (expo / jnp.sum(expo, axis=-1, keepdims=True)).astype(jnp.bfloat16)
    attended = jnp.einsum(
        "hqk,khd->qhd", probs, value_rows, preferred_element_type=jnp.float32
    ).astype(jnp.bfloat16)
    attended = attended.reshape(query_count, features)
    summed = jnp.dot(
        attended,
        lax.all_gather(out_weight, ("ha", "wa"), axis=0, tiled=True),
        preferred_element_type=jnp.float32,
    )
    result = summed.astype(jnp.bfloat16)
    return result.reshape(frame_count, row_count, column_count, D)


def solution(mesh):
    return jax.shard_map(
        shards,
        mesh=mesh,
        in_specs=(
            P("ta", "ha", "wa", None),
            P("ta", "ha", "wa", None),
            P("ta", "ha", "wa", None),
            P(),
            P(("ha", "wa"), None),
        ),
        out_specs=P("ta", "ha", "wa", None),
        check_vma=False,
    )
```

profile of v0, /device:TPU:168, one launch (start us, length us, event | category | flops | bytes accessed | tf_op | source)
XLA Modules:
  0.0 206.3 jit_solution(18270113067983858221)
XLA Ops:
  6.5 0.0 all-gather.2.cloned.1.call-start
  6.5 0.7 all-gather.2.cloned.1.call-update
  7.3 1.1 pad_maximum_fusion.8
  8.4 1.9 collective-permute-start
  10.3 5.8 %collective-permute-start.1 = (bf16[2,3,4,8,1536]{4,3,2,1,0:T(8,128)(2,1)S(1)}, bf16[2,3,4,8,1536]{4,3,2,1,0:T(8,128)(2,1)S(1)}, u32[]{:S(2)}, u32[]{:S(2)}) collective-permute-start(bf16[2,3,4,8,1536]{4,3,2,1,0:T(8,128)(2,1)S(1)} %pad_maximum_fusion.8), channel_id=1, source_target_pairs={{8,0},{16,8},{24,16},{32,24},{40,32},{48,40},{56,48},{9,1},{17,9},... | collective-permute-start | bytes 1769480 | tf_op jit(solution)/shard_map/ppermute | solution.py:20
  16.1 0.5 iota_add_fusion.2
  16.7 0.1 subtract_abs_fusion.1
  16.8 0.8 slice_bitcast_fusion.2
  17.6 1.9 reshape.315
  19.5 0.1 subtract_abs_fusion
  19.6 0.1 compare_and_fusion.1
  19.7 0.0 copy-start.5
  19.7 0.0 copy-start
  19.7 0.0 copy-start.1
  19.7 7.0 %collective-permute-done = bf16[2,3,4,8,1536]{4,3,2,1,0:T(8,128)(2,1)S(1)} collective-permute-done((bf16[2,3,4,8,1536]{4,3,2,1,0:T(8,128)(2,1)S(1)}, bf16[2,3,4,8,1536]{4,3,2,1,0:T(8,128)(2,1)S(1)}, u32[]{:S(2)}, u32[]{:S(2)}) %collective-permute-start) | collective-permute-done | bytes 589856 | tf_op jit(solution)/shard_map/ppermute | solution.py:17
  26.7 3.0 %collective-permute-done.1 = bf16[2,3,4,8,1536]{4,3,2,1,0:T(8,128)(2,1)S(1)} collective-permute-done((bf16[2,3,4,8,1536]{4,3,2,1,0:T(8,128)(2,1)S(1)}, bf16[2,3,4,8,1536]{4,3,2,1,0:T(8,128)(2,1)S(1)}, u32[]{:S(2)}, u32[]{:S(2)}) %collective-permute-start.1) | collective-permute-done | bytes 589856 | tf_op jit(solution)/shard_map/ppermute | solution.py:20
  29.7 1.2 pad_maximum_fusion.1
  30.9 0.7 fusion.24
  31.6 5.8 %collective-permute-start.2 = (bf16[2,3,12,4,1536]{4,3,2,1,0:T(4,128)(2,1)S(1)}, bf16[2,3,12,4,1536]{4,3,2,1,0:T(4,128)(2,1)S(1)}, u32[]{:S(2)}, u32[]{:S(2)}) collective-permute-start(bf16[2,3,12,4,1536]{4,3,2,1,0:T(4,128)(2,1)S(1)} %get-tuple-element.9), channel_id=1, source_target_pairs={{0,1},{1,2},{2,3},{3,4},{4,5},{5,6},{6,7},{8,9},{9,10},{10,11},{11... | collective-permute-start | bytes 2654216 | tf_op jit(solution)/shard_map/ppermute | solution.py:17
  37.4 1.9 collective-permute-start.3
  39.3 0.0 copy-done.5
  39.3 0.1 subtract_abs_fusion.2
  39.4 0.1 compare_and_fusion.2
  39.5 0.1 compare_and_fusion
  39.6 0.1 broadcast_and_fusion.1
  39.7 15.1 %collective-permute-done.2 = bf16[2,3,12,4,1536]{4,3,2,1,0:T(4,128)(2,1)S(1)} collective-permute-done((bf16[2,3,12,4,1536]{4,3,2,1,0:T(4,128)(2,1)S(1)}, bf16[2,3,12,4,1536]{4,3,2,1,0:T(4,128)(2,1)S(1)}, u32[]{:S(2)}, u32[]{:S(2)}) %collective-permute-start.2) | collective-permute-done | bytes 884768 | tf_op jit(solution)/shard_map/ppermute | solution.py:17
  54.8 5.1 %collective-permute-done.3 = bf16[2,3,12,4,1536]{4,3,2,1,0:T(4,128)(2,1)S(1)} collective-permute-done((bf16[2,3,12,4,1536]{4,3,2,1,0:T(4,128)(2,1)S(1)}, bf16[2,3,12,4,1536]{4,3,2,1,0:T(4,128)(2,1)S(1)}, u32[]{:S(2)}, u32[]{:S(2)}) %collective-permute-start.3) | collective-permute-done | bytes 884768 | tf_op jit(solution)/shard_map/ppermute | solution.py:20
  59.9 0.0 copy-done
  59.9 0.0 copy-done.1
  59.9 2.8 %pad_maximum_fusion.7 = (bf16[2,1,12,16,1536]{4,3,2,1,0:T(8,128)(2,1)}, bf16[2,1,12,16,1536]{4,3,2,1,0:T(8,128)(2,1)}) fusion(bf16[2,3,12,4,1536]{4,3,2,1,0:T(4,128)(2,1)S(1)} %collective-permute-done.3, bf16[2,3,12,4,1536]{4,3,2,1,0:T(4,128)(2,1)S(1)} %collective-permute-done.2, bf16[2,3,4,8,1536]{4,3,2,1,0:T(8,128)(2,1)S(1)} %collective-permute-done.1, ...), kind=kLoop, calls=%fused_computation.21 | loop fusion | flops 14155776 | bytes 5898240 | tf_op jit(solution)/shard_map/slice | solution.py:45
  62.7 9.6 %collective-permute-start.4 = (bf16[2,1,12,16,1536]{4,3,2,1,0:T(8,128)(2,1)}, bf16[2,1,12,16,1536]{4,3,2,1,0:T(8,128)(2,1)}, u32[]{:S(2)}, u32[]{:S(2)}) collective-permute-start(bf16[2,1,12,16,1536]{4,3,2,1,0:T(8,128)(2,1)} %get-tuple-element.7), channel_id=1, source_target_pairs={{0,64},{64,128},{128,192},{192,256},{256,320},{320,384},{384,448},... | collective-permute-start | bytes 3538952 | tf_op jit(solution)/shard_map/ppermute | solution.py:28
  72.3 2.1 %collective-permute-start.5 = (bf16[2,1,12,16,1536]{4,3,2,1,0:T(8,128)(2,1)}, bf16[2,1,12,16,1536]{4,3,2,1,0:T(8,128)(2,1)}, u32[]{:S(2)}, u32[]{:S(2)}) collective-permute-start(bf16[2,1,12,16,1536]{4,3,2,1,0:T(8,128)(2,1)} %get-tuple-element.8), channel_id=1, source_target_pairs={{64,0},{128,64},{192,128},{256,192},{320,256},{384,320},{448,384},... | collective-permute-start | bytes 3538952 | tf_op jit(solution)/shard_map/ppermute | solution.py:28
  74.4 7.1 %broadcast_and_fusion = pred[12,3,4,8,5,12,16]{6,5,4,3,2,1,0:T(8,128)(4,1)} fusion(pred[12,8,16]{2,1,0:T(8,128)(4,1)S(1)} %compare_and_fusion, pred[12,3,4,5,12]{4,3,2,1,0:T(8,128)(4,1)S(1)} %broadcast_and_fusion.1), kind=kLoop, calls=%fused_computation.1 | loop fusion | flops 1105920 | bytes 1116096 | tf_op jit(solution)/shard_map/and | solution.py:73
  81.5 20.0 %and.188 = pred[12,96,960]{2,1,0:T(32,128)(4,1)} reshape(pred[12,3,4,8,5,12,16]{6,5,4,3,2,1,0:T(8,128)(4,1)} %broadcast_and_fusion) | data formatting | bytes 2211840 | tf_op jit(solution)/shard_map/and | solution.py:73
  101.5 33.2 %collective-permute-done.4 = bf16[2,1,12,16,1536]{4,3,2,1,0:T(8,128)(2,1)} collective-permute-done((bf16[2,1,12,16,1536]{4,3,2,1,0:T(8,128)(2,1)}, bf16[2,1,12,16,1536]{4,3,2,1,0:T(8,128)(2,1)}, u32[]{:S(2)}, u32[]{:S(2)}) %collective-permute-start.4) | collective-permute-done | bytes 1179680 | tf_op jit(solution)/shard_map/ppermute | solution.py:28
  134.7 26.9 %collective-permute-done.5 = bf16[2,1,12,16,1536]{4,3,2,1,0:T(8,128)(2,1)} collective-permute-done((bf16[2,1,12,16,1536]{4,3,2,1,0:T(8,128)(2,1)}, bf16[2,1,12,16,1536]{4,3,2,1,0:T(8,128)(2,1)}, u32[]{:S(2)}, u32[]{:S(2)}) %collective-permute-start.5) | collective-permute-done | bytes 1179680 | tf_op jit(solution)/shard_map/ppermute | solution.py:28
  161.6 4.4 %pad_maximum_fusion = bf16[2,5,12,16,1536]{4,3,2,1,0:T(8,128)(2,1)S(1)} fusion(bf16[2,1,12,16,1536]{4,3,2,1,0:T(8,128)(2,1)} %collective-permute-done.5, bf16[2,3,12,4,1536]{4,3,2,1,0:T(4,128)(2,1)S(1)} %collective-permute-done.3, bf16[2,3,4,8,1536]{4,3,2,1,0:T(8,128)(2,1)S(1)} %collective-permute-done.1, bf16[1,3,4,8,1536]{4,3,2,1,0:T(8,128)(2,1)S(1)} %bitcast.36, ...), kind=kLoop, calls=%fused_computation.2 | loop fusion | flops 47185920 | bytes 11796480 | tf_op jit(solution)/shard_map/concatenate | solution.py:47
  166.1 2.2 %fusion.23 = (bf16[1,5,12,16,1536]{4,3,2,1,0:T(8,128)(2,1)}, bf16[1,5,12,16,1536]{4,3,2,1,0:T(8,128)(2,1)S(1)}) fusion(bf16[2,5,12,16,1536]{4,3,2,1,0:T(8,128)(2,1)S(1)} %pad_maximum_fusion), kind=kLoop, calls=%fused_computation.64 | loop fusion | bytes 11796480 | tf_op jit(solution)/shard_map/slice | solution.py:80
  168.3 6.5 %reshape_squeeze.7 = bf16[960,12,128]{2,1,0:T(8,128)(2,1)} reshape(bf16[1,5,12,16,1536]{4,3,2,1,0:T(8,128)(2,1)} %get-tuple-element.5) | data formatting | bytes 5898240 | tf_op jit(solution)/shard_map/reshape;squeeze | solution.py:80
  174.8 0.0 copy-start.3
  174.8 4.0 %reshape_squeeze.6 = bf16[960,12,128]{2,1,0:T(8,128)(2,1)} reshape(bf16[1,5,12,16,1536]{4,3,2,1,0:T(8,128)(2,1)S(1)} %get-tuple-element.6) | data formatting | bytes 5898240 | tf_op jit(solution)/shard_map/reshape;squeeze | solution.py:81
  178.8 0.0 copy-done.3
  178.8 0.0 copy-start.4
  178.8 4.0 %fusion.3 = f32[12,960,96]{1,2,0:T(8,128)S(1)} fusion(bf16[960,12,128]{2,1,0:T(8,128)(2,1)} %reshape_squeeze.7, bf16[96,12,128]{2,1,0:T(8,128)(2,1)S(1)} %copy-done.3), kind=kOutput, calls=%fused_computation.9 | convolution fusion | flops 283115520 | bytes 7667712 | tf_op jit(solution)/shard_map/qhd,khd->hqk/dot_general | solution.py:82
  182.9 0.0 copy-start.2
  182.9 2.1 %copy-done.2 = f32[12,960,96]{1,2,0:T(8,128)} copy-done((f32[12,960,96]{1,2,0:T(8,128)}, f32[12,960,96]{1,2,0:T(8,128)S(1)}, u32[]{:S(2)}) %copy-start.2) | copy-done | bytes 4423704
  185.0 0.0 copy-done.4
  185.0 1.7 fusion.25
  186.7 6.6 %fusion.11 = bf16[12,12,8,128]{3,2,1,0:T(8,128)(2,1)S(1)} fusion(bf16[960,12,128]{2,1,0:T(8,128)(2,1)} %reshape_squeeze.6, f32[12,96]{1,0:T(8,128)S(1)} %fusion.25, pred[12,96,960]{2,1,0:T(32,128)(4,1)S(1)} %copy-done.4, f32[12,960,96]{1,2,0:T(8,128)} %copy-done.2), kind=kOutput, calls=%fused_computation.22 | convolution fusion | flops 288794688 | bytes 8778240 | tf_op jit(solution)/shard_map/hqk,khd->qhd/dot_general | solution.py:89
  193.3 0.0 all-gather.2.cloned.1.call-done
  193.3 6.1 %convolution_convert_fusion = bf16[96,3072]{1,0:T(8,128)(2,1)} fusion(bf16[1536,3072]{1,0:T(8,128)(2,1)} %all-gather.2.cloned.1.call-done, bf16[12,12,8,128]{3,2,1,0:T(8,128)(2,1)S(1)} %fusion.11), kind=kOutput, calls=%fused_computation.6 | convolution fusion | flops 906264576 | bytes 10321920 | tf_op jit(solution)/shard_map/dot_general | solution.py:93
  (8 shorter events, 0.1 us)
Async XLA Ops:
  6.5 186.8 %all-gather.2.cloned.1.call-start = ((), (), s32[]{:S(2)}) async-start(), calls=%async_computation | async-start | bytes 9584640 | tf_op jit(solution)/shard_map/all_gather | solution.py:95
  8.4 18.3 %collective-permute-start = (bf16[2,3,4,8,1536]{4,3,2,1,0:T(8,128)(2,1)S(1)}, bf16[2,3,4,8,1536]{4,3,2,1,0:T(8,128)(2,1)S(1)}, u32[]{:S(2)}, u32[]{:S(2)}) collective-permute-start(bf16[2,3,4,8,1536]{4,3,2,1,0:T(8,128)(2,1)S(1)} %pad_maximum_fusion.8), channel_id=1, source_target_pairs={{0,8},{8,16},{16,24},{24,32},{32,40},{40,48},{48,56},{1,9},{9,17},... | collective-permute-start | bytes 1769480 | tf_op jit(solution)/shard_map/ppermute | solution.py:17
  10.3 19.4 %collective-permute-start.1 = (bf16[2,3,4,8,1536]{4,3,2,1,0:T(8,128)(2,1)S(1)}, bf16[2,3,4,8,1536]{4,3,2,1,0:T(8,128)(2,1)S(1)}, u32[]{:S(2)}, u32[]{:S(2)}) collective-permute-start(bf16[2,3,4,8,1536]{4,3,2,1,0:T(8,128)(2,1)S(1)} %pad_maximum_fusion.8), channel_id=1, source_target_pairs={{8,0},{16,8},{24,16},{32,24},{40,32},{48,40},{56,48},{9,1},{17,9},... | collective-permute-start | bytes 1769480 | tf_op jit(solution)/shard_map/ppermute | solution.py:20
  19.7 19.7 %copy-start.5 = (s32[5]{0:T(128)S(1)}, s32[5]{0:T(128)}, u32[]{:S(2)}) copy-start(s32[5]{0:T(128)} %iota_add_fusion.2) | copy-start | bytes 64
  19.7 40.3 %copy-start = (bf16[3,4,8,1536]{3,2,1,0:T(8,128)(2,1)S(1)}, bf16[3,4,8,1536]{3,2,1,0:T(8,128)(2,1)}, u32[]{:S(2)}) copy-start(bf16[3,4,8,1536]{3,2,1,0:T(8,128)(2,1)} %param.7) | copy-start | bytes 884740
  19.7 40.2 %copy-start.1 = (bf16[3,4,8,1536]{3,2,1,0:T(8,128)(2,1)S(1)}, bf16[3,4,8,1536]{3,2,1,0:T(8,128)(2,1)}, u32[]{:S(2)}) copy-start(bf16[3,4,8,1536]{3,2,1,0:T(8,128)(2,1)} %param.6) | copy-start | bytes 884740
  31.6 23.2 %collective-permute-start.2 = (bf16[2,3,12,4,1536]{4,3,2,1,0:T(4,128)(2,1)S(1)}, bf16[2,3,12,4,1536]{4,3,2,1,0:T(4,128)(2,1)S(1)}, u32[]{:S(2)}, u32[]{:S(2)}) collective-permute-start(bf16[2,3,12,4,1536]{4,3,2,1,0:T(4,128)(2,1)S(1)} %get-tuple-element.9), channel_id=1, source_target_pairs={{0,1},{1,2},{2,3},{3,4},{4,5},{5,6},{6,7},{8,9},{9,10},{10,11},{11... | collective-permute-start | bytes 2654216 | tf_op jit(solution)/shard_map/ppermute | solution.py:17
  37.4 22.5 %collective-permute-start.3 = (bf16[2,3,12,4,1536]{4,3,2,1,0:T(4,128)(2,1)S(1)}, bf16[2,3,12,4,1536]{4,3,2,1,0:T(4,128)(2,1)S(1)}, u32[]{:S(2)}, u32[]{:S(2)}) collective-permute-start(bf16[2,3,12,4,1536]{4,3,2,1,0:T(4,128)(2,1)S(1)} %get-tuple-element.10), channel_id=1, source_target_pairs={{1,0},{2,1},{3,2},{4,3},{5,4},{6,5},{7,6},{9,8},{10,9},{11,10},{12... | collective-permute-start | bytes 2654216 | tf_op jit(solution)/shard_map/ppermute | solution.py:20
  62.7 72.0 %collective-permute-start.4 = (bf16[2,1,12,16,1536]{4,3,2,1,0:T(8,128)(2,1)}, bf16[2,1,12,16,1536]{4,3,2,1,0:T(8,128)(2,1)}, u32[]{:S(2)}, u32[]{:S(2)}) collective-permute-start(bf16[2,1,12,16,1536]{4,3,2,1,0:T(8,128)(2,1)} %get-tuple-element.7), channel_id=1, source_target_pairs={{0,64},{64,128},{128,192},{192,256},{256,320},{320,384},{384,448},... | collective-permute-start | bytes 3538952 | tf_op jit(solution)/shard_map/ppermute | solution.py:28
  72.3 89.3 %collective-permute-start.5 = (bf16[2,1,12,16,1536]{4,3,2,1,0:T(8,128)(2,1)}, bf16[2,1,12,16,1536]{4,3,2,1,0:T(8,128)(2,1)}, u32[]{:S(2)}, u32[]{:S(2)}) collective-permute-start(bf16[2,1,12,16,1536]{4,3,2,1,0:T(8,128)(2,1)} %get-tuple-element.8), channel_id=1, source_target_pairs={{64,0},{128,64},{192,128},{256,192},{320,256},{384,320},{448,384},... | collective-permute-start | bytes 3538952 | tf_op jit(solution)/shard_map/ppermute | solution.py:28
  174.8 4.0 %copy-start.3 = (bf16[96,12,128]{2,1,0:T(8,128)(2,1)S(1)}, bf16[96,12,128]{2,1,0:T(8,128)(2,1)}, u32[]{:S(2)}) copy-start(bf16[96,12,128]{2,1,0:T(8,128)(2,1)} %reshape.315) | copy-start | bytes 884740
  178.8 6.2 %copy-start.4 = (pred[12,96,960]{2,1,0:T(32,128)(4,1)S(1)}, pred[12,96,960]{2,1,0:T(32,128)(4,1)}, u32[]{:S(2)}) copy-start(pred[12,96,960]{2,1,0:T(32,128)(4,1)} %and.188) | copy-start | bytes 3317764
  182.9 2.1 %copy-start.2 = (f32[12,960,96]{1,2,0:T(8,128)}, f32[12,960,96]{1,2,0:T(8,128)S(1)}, u32[]{:S(2)}) copy-start(f32[12,960,96]{1,2,0:T(8,128)S(1)} %fusion.3) | copy-start | bytes 13271044
Sparse Core Ops, SparseCore 0:
  10.7 123.4 all-gather.1
where the time goes:
time: 207 us; the launch traced here: 206 us
  waiting for transfers between devices  91 us (44%)
  local copies, waits for them, and re-layouts  38.4 us (19%)
  starting transfers between devices  27 us (13%)
  other arithmetic  19.6 us (9%)
  matrix products  16.7 us (8%)
  between operations  13.6 us (7%)
    ppermute x2, waiting for transfers between devices, shifted(): lax.ppermute(value, axis, [(source, source + steps) for source in range(i...  60.1 us
    ppermute x2, waiting for transfers between devices, padded(): lax.ppermute(lax.slice_in_dim(block, block.shape[dim] - width, None, axis...  22.1 us
    and x1, local copies, waits for them, and re-layouts, shards(): allow_t[:, :, None, None, :, None, None]  20 us
    ppermute x2, starting transfers between devices, shifted(): lax.ppermute(value, axis, [(source, source + steps) for source in range(i...  11.7 us
    ppermute x2, waiting for transfers between devices, padded(): lax.ppermute(lax.slice_in_dim(block, 0, width, axis=dim), axis, backward)  8.04 us
    ppermute x2, starting transfers between devices, padded(): lax.ppermute(lax.slice_in_dim(block, block.shape[dim] - width, None, axis...  7.69 us
    ppermute x2, starting transfers between devices, padded(): lax.ppermute(lax.slice_in_dim(block, 0, width, axis=dim), axis, backward)  7.67 us
    and x2, other arithmetic, shards(): allow_t[:, :, None, None, :, None, None]  7.21 us
  transfers between devices with their start and end apart: 7, of which 6 were waited for; matrix products, arithmetic and copies ran while one was open for 32% of the time, Pallas kernels for 0%

commit v1 on v0

v1 whole, which is shorter than its diff:
```python
import math

import jax
import jax.numpy as jnp
from jax import lax
from jax.experimental import pallas as pl
from jax.experimental.pallas import tpu as pltpu
from jax.sharding import PartitionSpec as P

D = 3072
TILE = 4
HEADS = 12
HEAD_DIM = 128
R = HEADS * HEAD_DIM
CHUNKS = 4
PER_CHUNK = HEADS // CHUNKS
NA = 8
FRAMES_HERE = 3
TOKENS = 96
ROWS_W = 24
HALF = D // 2
PIECE = D // 4
COLS = 512
MESH = pl.DeviceIdType.MESH


def kernel(q_ref, k_ref, v_ref, rad_ref, w_ref, o_ref, kv, wbuf, code, att, send_sems, recv_sems, local_sem):
    ta, ha, wa = lax.axis_index("ta"), lax.axis_index("ha"), lax.axis_index("wa")
    core = lax.rem(ha, 2)
    par = lax.rem(lax.div(ta, 2), 2)

    def step(pos, by):
        return lax.rem(pos + (by + NA), NA)

    partner = ha + 1 - 2 * core

    barrier = pltpu.get_barrier_semaphore()
    greet = [{"ta": step(ta, d)} for d in (1, -1, 2, -2)]
    greet += [{"ha": step(ha, d)} for d in range(1, NA)]
    greet += [{"wa": step(wa, d)} for d in (1, -1)]
    for who in greet:
        pl.semaphore_signal(barrier, inc=1, device_id=who, device_id_type=MESH)

    to = lax.broadcasted_iota(jnp.int32, (TOKENS, TOKENS), 0)
    come = lax.broadcasted_iota(jnp.int32, (TOKENS, TOKENS), 1)
    frame, left = to // 32, to % 32
    source = frame * 32 + ((left % 16) // 4) * 8 + (left // 16) * 4 + left % 4
    order = (source == come).astype(jnp.bfloat16)
    for which, ref in ((0, k_ref), (1, v_ref)):
        moved = jnp.dot(order, ref[...], preferred_element_type=jnp.float32).astype(jnp.bfloat16)
        for head in range(HEADS):
            part = moved[:, head * HEAD_DIM : (head + 1) * HEAD_DIM]
            kv[head, which, 1:4, 1, 1:3] = part.reshape(FRAMES_HERE, 2, 16, HEAD_DIM)

    pl.semaphore_wait(barrier, len(greet))

    started = []

    def send(src, dst, who):
        i = len(started)
        copy = pltpu.make_async_remote_copy(
            src_ref=src, dst_ref=dst, send_sem=send_sems.at[i], recv_sem=recv_sems.at[i],
            device_id=who, device_id_type=MESH,
        )
        copy.start()
        started.append(copy)
        return copy

    def piece(parity, which_core):
        return pl.ds(pl.multiple_of(which_core * HALF + parity * PIECE, 128), PIECE)

    mine = piece(par, core)

    def heads_of(c):
        return pl.ds(c * PER_CHUNK, PER_CHUNK)

    own = pltpu.make_async_copy(w_ref.at[:, mine], wbuf.at[ha, wa, :, mine], local_sem)
    own.start()

    def send_t(c):
        h = heads_of(c)
        return [
            send(kv.at[h, :, 3, 1, 1:3], kv.at[h, :, 0, 1, 1:3], {"ta": step(ta, 1)}),
            send(kv.at[h, :, 1, 1, 1:3], kv.at[h, :, 4, 1, 1:3], {"ta": step(ta, -1)}),
        ]

    t_copies = [send_t(0)]
    y_copies = []
    for d in range(1, NA):
        other = step(ha, d)
        cols = piece(par, lax.rem(other, 2))
        y_copies.append(send(w_ref.at[:, cols], wbuf.at[ha, wa, :, cols], {"ha": other}))
    t_copies += [send_t(c) for c in range(1, CHUNKS)]

    def send_h(c):
        for copy in t_copies[c]:
            copy.wait_recv()
        h = heads_of(c)
        return [
            send(kv.at[h, :, :, 1, 1:3], kv.at[h, :, :, 0, 1:3], {"ha": step(ha, 1)}),
            send(kv.at[h, :, :, 1, 1:3], kv.at[h, :, :, 2, 1:3], {"ha": step(ha, -1)}),
        ]

    def send_w(c):
        for copy in h_copies[c]:
            copy.wait_recv()
        h = heads_of(c)
        rows = pl.ds(core, 2)
        return [
            send(kv.at[h, :, :, rows, 2], kv.at[h, :, :, rows, 0], {"wa": step(wa, 1)}),
            send(kv.at[h, :, :, rows, 1], kv.at[h, :, :, rows, 3], {"wa": step(wa, -1)}),
        ]

    def send_c(c):
        for copy in w_copies[c]:
            copy.wait_recv()
        h = heads_of(c)
        there = 2 * core
        return [
            send(kv.at[h, :, :, 1, 0], kv.at[h, :, :, there, 0], {"ha": partner}),
            send(kv.at[h, :, :, 1, 3], kv.at[h, :, :, there, 3], {"ha": partner}),
        ]

    def ring_up(r):
        at = step(wa, 1 - r)
        return send(wbuf.at[:, at, :, mine], wbuf.at[:, at, :, mine], {"wa": step(wa, 1)})

    def ring_down(r):
        at = step(wa, r - 1)
        return send(wbuf.at[:, at, :, mine], wbuf.at[:, at, :, mine], {"wa": step(wa, -1)})

    def send_x(at):
        return [
            send(wbuf.at[4:8, at, :, mine], wbuf.at[4:8, at, :, mine], {"ta": step(ta, 2)}),
            send(wbuf.at[0:4, at, :, mine], wbuf.at[0:4, at, :, mine], {"ta": step(ta, -2)}),
        ]

    def send_pair(block):
        at, copies = block
        for copy in copies:
            copy.wait_recv()
        cols = pl.ds(pl.multiple_of(core * HALF, 128), HALF)
        return send(wbuf.at[:, at, :, cols], wbuf.at[:, at, :, cols], {"ha": partner})

    def attend(c):
        for copy in c_copies[c]:
            copy.wait_recv()

        @pl.loop(0, PER_CHUNK)
        def _(i):
            head = c * PER_CHUNK + i
            lanes = pl.ds(pl.multiple_of(head * HEAD_DIM, 128), HEAD_DIM)
            closed = 8
            for axis in range(3):
                closed = closed + jnp.where(rad_ref[head, axis] == 0, 1 << axis, 0)
            for f in range(FRAMES_HERE):
                q = q_ref[f * 32 : (f + 1) * 32, lanes]
                k = kv[head, 0, f : f + 3].reshape(576, HEAD_DIM)
                v = kv[head, 1, f : f + 3].reshape(576, HEAD_DIM)
                s = lax.dot_general(q, k, (((1,), (1,)), ((), ())), preferred_element_type=jnp.float32)
                s = s * (1.0 / math.sqrt(HEAD_DIM))
                s = jnp.where((code[f] & closed) == 0, s, -jnp.inf)
                biggest = jnp.max(s, axis=-1, keepdims=True)
                expo = jnp.exp(s - biggest)
                probs = (expo / jnp.sum(expo, axis=-1, keepdims=True)).astype(jnp.bfloat16)
                out = jnp.dot(probs, v, preferred_element_type=jnp.float32)
                att[f * 32 : (f + 1) * 32, lanes] = out.astype(jnp.bfloat16)

    qi = lax.broadcasted_iota(jnp.int32, (32, 576), 0)
    kj = lax.broadcasted_iota(jnp.int32, (32, 576), 1)
    dt = kj // 192 - 1
    dh = (kj % 192) // 64 - 1
    wj = (kj % 64) // 16
    dw = jnp.abs(wj - 1 - (qi % 8) // 4)
    row_at, col_at = ha + dh, 2 * wa + wj - 1
    never = (dw > 1) | (row_at < 0) | (row_at >= NA) | (col_at < 0) | (col_at >= 2 * NA)
    kind = jnp.where(dt == 0, 0, 1) + jnp.where(dh == 0, 0, 2) + jnp.where(dw == 0, 0, 4)
    for f in range(FRAMES_HERE):
        frame_at = FRAMES_HERE * ta + f + dt
        out_of = never | (frame_at < 0) | (frame_at >= FRAMES_HERE * NA)
        code[f] = kind + jnp.where(out_of, 8, 0)

    h_copies = [send_h(0)]
    own.wait()
    for copy in y_copies:
        copy.wait_recv()
    blocks = []
    up, down = [ring_up(1)], [ring_down(1)]
    blocks.append((wa, send_x(wa)))
    h_copies.append(send_h(1))
    h_copies.append(send_h(2))
    h_copies.append(send_h(3))

    w_copies, c_copies, pair_copies = [], [], []

    def next_ring(r):
        up[-1].wait_recv()
        if r < 4:
            up.append(ring_up(r + 1))
        blocks.append((step(wa, -r), send_x(step(wa, -r))))
        if r < 4:
            down[-1].wait_recv()
            if r < 3:
                down.append(ring_down(r + 1))
            blocks.append((step(wa, r), send_x(step(wa, r))))

    w_copies.append(send_w(0))
    next_ring(1)
    w_copies.append(send_w(1))
    c_copies.append(send_c(0))
    next_ring(2)
    w_copies.append(send_w(2))
    c_copies.append(send_c(1))
    attend(0)
    next_ring(3)
    w_copies.append(send_w(3))
    pair_copies.append(send_pair(blocks[0]))
    c_copies.append(send_c(2))
    attend(1)
    next_ring(4)
    pair_copies.append(send_pair(blocks[1]))
    pair_copies.append(send_pair(blocks[2]))
    c_copies.append(send_c(3))
    attend(2)
    pair_copies.append(send_pair(blocks[3]))
    pair_copies.append(send_pair(blocks[4]))
    attend(3)
    for block in blocks[5:]:
        pair_copies.append(send_pair(block))

    def project(which_core):
        @pl.loop(0, HALF // COLS)
        def _(n):
            cols = pl.ds(pl.multiple_of(which_core * HALF + n * COLS, 128), COLS)
            w = wbuf[:, :, :, cols].reshape(R, COLS)
            o_ref[:, cols] = jnp.dot(att[...], w, preferred_element_type=jnp.float32).astype(jnp.bfloat16)

    project(core)
    for copy in pair_copies:
        copy.wait_recv()
    project(1 - core)
    for copy in started:
        copy.wait_send()


COPIES = 8 * CHUNKS + 7 + 7 + 16 + 8


def shards(queries, keys, values, radius, out_weight):
    shape = queries.shape[:3]
    vmem = pl.BlockSpec(memory_space=pltpu.VMEM)
    out = pl.pallas_call(
        kernel,
        out_shape=jax.ShapeDtypeStruct((TOKENS, D), jnp.bfloat16),
        in_specs=[vmem, vmem, vmem, pl.BlockSpec(memory_space=pltpu.SMEM), vmem],
        out_specs=vmem,
        scratch_shapes=[
            pltpu.VMEM((HEADS, 2, 5, 3, 4, 16, HEAD_DIM), jnp.bfloat16),
            pltpu.VMEM((NA, NA, ROWS_W, D), jnp.bfloat16),
            pltpu.VMEM((FRAMES_HERE, 32, 576), jnp.int32),
            pltpu.VMEM((TOKENS, R), jnp.bfloat16),
            pltpu.SemaphoreType.DMA((COPIES,)),
            pltpu.SemaphoreType.DMA((COPIES,)),
            pltpu.SemaphoreType.DMA,
        ],
        compiler_params=pltpu.CompilerParams(
            collective_id=0, has_side_effects=True, vmem_limit_bytes=48 * 1024 * 1024
        ),
    )(
        queries.reshape(TOKENS, R),
        keys.reshape(TOKENS, R),
        values.reshape(TOKENS, R),
        radius,
        out_weight,
    )
    return out.reshape(*shape, D)


def solution(mesh):
    return jax.shard_map(
        shards,
        mesh=mesh,
        in_specs=(
            P("ta", "ha", "wa", None),
            P("ta", "ha", "wa", None),
            P("ta", "ha", "wa", None),
            P(),
            P(("ha", "wa"), None),
        ),
        out_specs=P("ta", "ha", "wa", None),
        check_vma=False,
    )
```

time: 207 us -> 103 us (0.50)
  the two profiles are of different devices: /device:TPU:168 before, /device:TPU:1 now
where the time goes in v1:
time: 103 us; the launch traced here: 102 us
  Pallas kernels  96.9 us (94%)
  local copies, waits for them, and re-layouts  5.39 us (5%)
    pallas_call x1, Pallas kernels, shards(): pl.pallas_call(kernel, out_shape=jax.ShapeDtypeStruct((TOKENS, D), jnp.bf...  96.9 us
    unnamed x12, local copies, waits for them, and re-layouts  5.39 us

profile of v1, /device:TPU:1, one launch (start us, length us, event | category | flops | bytes accessed | tf_op | source)
XLA Modules:
  0.0 102.3 jit_solution(18132456477088126363)
XLA Ops:
  0.0 0.0 copy-start.4
  0.0 0.7 copy-done.4
  0.7 0.1 copy.6.rad_ref
  0.8 0.0 copy-start
  0.8 1.0 copy-done
  1.7 0.0 copy-start.1
  1.7 1.0 copy-done.1
  2.7 0.0 copy-start.2
  2.7 1.0 copy-done.2
  3.7 0.0 copy-start.3
  3.7 0.9 copy-done.3
  4.6 96.9 %shard_map.55 = bf16[96,3072]{1,0:T(8,128)(2,1)S(1)} custom-call(bf16[96,1536]{1,0:T(8,128)(2,1)S(1)} %bitcast.5, bf16[96,1536]{1,0:T(8,128)(2,1)S(1)} %bitcast.6, bf16[96,1536]{1,0:T(8,128)(2,1)S(1)} %bitcast.7, s32[12,3]{1,0:T(8,128)S(1)} %copy.6.rad_ref, bf16[24,3072]{1,0:T(8,128)(2,1)S(1)} %copy-done.3), custom_call_target="tpu_custom_call" | custom-call | tf_op jit(solution)/shard_map/pallas_call | solution.py:252
  101.5 0.8 copy.8
Async XLA Ops:
  0.0 0.7 copy-start.4
  0.8 1.0 copy-start
  1.7 1.0 copy-start.1
  2.7 1.0 copy-start.2
  3.7 0.9 copy-start.3

commit v2 on v1

v2 whole, which is shorter than its diff:
```python
import math

import jax
import jax.numpy as jnp
from jax import lax
from jax.experimental import pallas as pl
from jax.experimental.pallas import tpu as pltpu
from jax.sharding import PartitionSpec as P

D = 3072
TILE = 4
HEADS = 12
HEAD_DIM = 128
R = HEADS * HEAD_DIM
CHUNKS = ((0, 4), (4, 3), (7, 3), (10, 2))
NA = 8
FRAMES_HERE = 3
TOKENS = 96
ROWS_W = 24
HALF = D // 2
PIECE = D // 4
COLS = 512
COPIES = 96
MESH = pl.DeviceIdType.MESH


def kernel(
    q_hbm, k_hbm, v_hbm, rad_ref, w_hbm, o_ref,
    q_ref, k_ref, v_ref, w_ref, kv, wbuf, code, att, send_sems, recv_sems, local_sems,
):
    loads = [
        pltpu.make_async_copy(src, dst, local_sems.at[i])
        for i, (src, dst) in enumerate(((k_hbm, k_ref), (v_hbm, v_ref), (w_hbm, w_ref), (q_hbm, q_ref)))
    ]
    for load in loads:
        load.start()

    ta, ha, wa = lax.axis_index("ta"), lax.axis_index("ha"), lax.axis_index("wa")
    core = lax.rem(ha, 2)
    par = lax.rem(lax.div(ta, 2), 2)

    def step(pos, by):
        return lax.rem(pos + (by + NA), NA)

    partner = ha + 1 - 2 * core
    outer = 2 * core

    other_core = {"ha": partner}
    odd = lax.rem(ta, 2)
    twin = ta + 1 - 2 * odd
    away = 2 * odd - 1

    def chip_at(by, e):
        return lax.rem(lax.div(ha, 2) + by + NA, NA // 2) * 2 + lax.rem(core + e, 2)

    barrier = pltpu.get_barrier_semaphore()
    greet = [{"ta": step(ta, d)} for d in (1, -1, 2, -2)]
    greet += [{"wa": step(wa, d)} for d in (1, -1)]
    greet += [other_core]
    greet += [{"ha": chip_at(by, e)} for by in (1, -1) for e in (0, 1)]
    greet += [{"ta": twin, "ha": chip_at(by * away, e)} for by in (1, 2) for e in (0, 1)]
    for who in greet:
        pl.semaphore_signal(barrier, inc=1, device_id=who, device_id_type=MESH)

    to = lax.broadcasted_iota(jnp.int32, (TOKENS, TOKENS), 0)
    come = lax.broadcasted_iota(jnp.int32, (TOKENS, TOKENS), 1)
    frame, left = to // 32, to % 32
    source = frame * 32 + ((left % 16) // 4) * 8 + (left // 16) * 4 + left % 4
    order = (source == come).astype(jnp.bfloat16)
    for which, ref in ((0, k_ref), (1, v_ref)):
        loads[which].wait()
        moved = jnp.dot(order, ref[...], preferred_element_type=jnp.float32).astype(jnp.bfloat16)
        for head in range(HEADS):
            part = moved[:, head * HEAD_DIM : (head + 1) * HEAD_DIM]
            kv[head, which, 1:4, 1, 1:3] = part.reshape(FRAMES_HERE, 2, 16, HEAD_DIM)
    loads[2].wait()

    pl.semaphore_wait(barrier, len(greet))

    started = []

    def send(src, dst, who):
        i = len(started)
        copy = pltpu.make_async_remote_copy(
            src_ref=src, dst_ref=dst, send_sem=send_sems.at[i], recv_sem=recv_sems.at[i],
            device_id=who, device_id_type=MESH,
        )
        copy.start()
        started.append(copy)
        return copy

    def arrived(copies):
        for copy in copies:
            copy.wait_recv()

    def piece(parity, which_core):
        return pl.ds(pl.multiple_of(which_core * HALF + parity * PIECE, 128), PIECE)

    mine = piece(par, core)
    ta_up, ta_down = {"ta": step(ta, 1)}, {"ta": step(ta, -1)}
    ha_up, ha_down = {"ha": step(ha, 1)}, {"ha": step(ha, -1)}
    wa_up, wa_down = {"wa": step(wa, 1)}, {"wa": step(wa, -1)}

    y_copies = []
    for where in ({"ta": twin, "ha": 1}, {"ta": ta, "ha": 1}, {"ta": twin, "ha": 2}):
        for e in (0, 1):
            there = {"ta": where["ta"], "ha": chip_at(where["ha"] * away, e)}
            cols = piece(par, lax.rem(core + e, 2))
            y_copies.append(send(w_ref.at[:, cols], wbuf.at[ha, wa, :, cols], there))
    cols = piece(par, 1 - core)
    y_copies.append(send(w_ref.at[:, cols], wbuf.at[ha, wa, :, cols], other_core))
    own = pltpu.make_async_copy(w_ref.at[:, mine], wbuf.at[ha, wa, :, mine], local_sems.at[4])
    own.start()

    def rim(frames):
        return [
            send(kv.at[:, :, frames, 1, 2], kv.at[:, :, frames, 1, 0], wa_up),
            send(kv.at[:, :, frames, 1, 1], kv.at[:, :, frames, 1, 3], wa_down),
        ]

    def rim_across(frames):
        return [
            send(kv.at[:, :, frames, 1, 0], kv.at[:, :, frames, outer, 0], other_core),
            send(kv.at[:, :, frames, 1, 3], kv.at[:, :, frames, outer, 3], other_core),
        ]

    def rows(c, frames):
        first, count = CHUNKS[c]
        src = kv.at[pl.ds(first, count), :, frames, 1, 1:3]
        return [
            send(src, kv.at[pl.ds(first, count), :, frames, 0, 1:3], ha_up),
            send(src, kv.at[pl.ds(first, count), :, frames, 2, 1:3], ha_down),
        ]

    def outer_rim(c):
        arrived(h_copies[c])
        heads = pl.ds(CHUNKS[c][0], CHUNKS[c][1])
        return [
            send(kv.at[heads, :, :, outer, 2], kv.at[heads, :, :, outer, 0], wa_up),
            send(kv.at[heads, :, :, outer, 1], kv.at[heads, :, :, outer, 3], wa_down),
        ]

    OWN = slice(1, 4)
    w_own = rim(OWN)
    t_copies = [
        send(kv.at[:, :, 3, 1, 1:3], kv.at[:, :, 0, 1, 1:3], ta_up),
        send(kv.at[:, :, 1, 1, 1:3], kv.at[:, :, 4, 1, 1:3], ta_down),
    ]
    h_copies = [rows(0, OWN)]

    qi = lax.broadcasted_iota(jnp.int32, (TOKENS, 960), 0)
    kj = lax.broadcasted_iota(jnp.int32, (TOKENS, 960), 1)
    dt = jnp.abs(kj // 192 - 1 - qi // 32)
    dh = (kj % 192) // 64 - 1
    wj = (kj % 64) // 16
    dw = jnp.abs(wj - 1 - (qi % 8) // 4)
    row_at, col_at = ha + dh, 2 * wa + wj - 1
    frame_at = FRAMES_HERE * ta + kj // 192 - 1
    never = (dw > 1) | (dt > 1) | (row_at < 0) | (row_at >= NA) | (col_at < 0) | (col_at >= 2 * NA)
    never = never | (frame_at < 0) | (frame_at >= FRAMES_HERE * NA)
    kind = jnp.where(dt == 0, 0, 1) + jnp.where(dh == 0, 0, 2) + jnp.where(dw == 0, 0, 4)
    code[...] = kind + jnp.where(never, 8, 0)

    x_copies, pair_copies = {}, []

    def block(half, at, cols):
        return wbuf.at[4 * half : 4 * half + 4, at, :, cols]

    def ring(half, way, r):
        at = step(wa, way * (1 - r))
        return send(block(half, at, mine), block(half, at, mine), wa_up if way == 1 else wa_down)

    def across_x(half, at, key):
        x_copies[key, half] = at, send(
            block(half, at, mine), block(half, at, mine), {"ta": step(ta, 2 if half else -2)}
        )

    def to_partner(key, half):
        at, copy = x_copies[key, half]
        copy.wait_recv()
        cols = pl.ds(pl.multiple_of(core * HALF, 128), HALF)
        pair_copies.append(send(block(half, at, cols), block(half, at, cols), other_core))

    own.wait()
    arrived(y_copies)
    rings = {}
    for half in (0, 1):
        for way in (1, -1):
            rings[half, way, 1] = ring(half, way, 1)
        across_x(half, wa, 0)

    def next_ring(r, halves=(0, 1)):
        for half in halves:
            for way in (1, -1):
                if (half, way, r) not in rings:
                    continue
                rings[half, way, r].wait_recv()
                if r < 3 or (r == 3 and way == 1 - 2 * half):
                    rings[half, way, r + 1] = ring(half, way, r + 1)
                across_x(half, step(wa, -way * r), way * r if r < 4 else 4)

    def attend(c):
        arrived(o_copies[c])

        @pl.loop(0, CHUNKS[c][1])
        def _(i):
            head = CHUNKS[c][0] + i
            lanes = pl.ds(pl.multiple_of(head * HEAD_DIM, 128), HEAD_DIM)
            closed = 8
            for axis in range(3):
                closed = closed + jnp.where(rad_ref[axis, head] == 0, 1 << axis, 0)
            k = kv[head, 0].reshape(960, HEAD_DIM)
            v = kv[head, 1].reshape(960, HEAD_DIM)
            s = lax.dot_general(q_ref[:, lanes], k, (((1,), (1,)), ((), ())), preferred_element_type=jnp.float32)
            s = s * (1.0 / math.sqrt(HEAD_DIM))
            s = jnp.where((code[...] & closed) == 0, s, -jnp.inf)
            biggest = jnp.max(s, axis=-1, keepdims=True)
            expo = jnp.exp(s - biggest)
            probs = (expo * (1.0 / jnp.sum(expo, axis=-1, keepdims=True))).astype(jnp.bfloat16)
            out = jnp.dot(probs, v, preferred_element_type=jnp.float32)
            att[:, lanes] = out.astype(jnp.bfloat16)

    ALL = slice(0, 5)
    arrived(w_own)
    c_copies = rim_across(OWN)
    next_ring(1, (0,))
    arrived(t_copies)
    h_copies[0] = h_copies[0] + rows(0, 0) + rows(0, 4)
    h_copies += [rows(c, ALL) for c in range(1, len(CHUNKS))]
    w_t = [rim(0), rim(4)]
    next_ring(1, (1,))
    next_ring(2)
    o_copies = [outer_rim(0)]
    for copies, f in zip(w_t, (0, 4)):
        arrived(copies)
        c_copies += rim_across(f)
    to_partner(0, 0)
    to_partner(0, 1)
    next_ring(3, (0,))
    o_copies.append(outer_rim(1))
    next_ring(3, (1,))
    loads[3].wait()
    arrived(c_copies)
    o_copies.append(outer_rim(2))
    for key in (1, -1):
        to_partner(key, 0)
        to_partner(key, 1)
    next_ring(4)
    o_copies.append(outer_rim(3))
    attend(0)
    for key in (2, -2):
        to_partner(key, 0)
        to_partner(key, 1)
    attend(1)
    for key in (3, -3, 4):
        to_partner(key, 0)
        to_partner(key, 1)
    attend(2)
    attend(3)

    def project(which_core):
        @pl.loop(0, HALF // COLS)
        def _(n):
            cols = pl.ds(pl.multiple_of(which_core * HALF + n * COLS, 128), COLS)
            w = wbuf[:, :, :, cols].reshape(R, COLS)
            o_ref[:, cols] = jnp.dot(att[...], w, preferred_element_type=jnp.float32).astype(jnp.bfloat16)

    project(core)
    arrived(pair_copies)
    project(1 - core)
    for copy in started:
        copy.wait_send()


def shards(queries, keys, values, radius, out_weight):
    shape = queries.shape[:3]
    hbm = pl.BlockSpec(memory_space=pltpu.HBM)
    out = pl.pallas_call(
        kernel,
        out_shape=jax.ShapeDtypeStruct((TOKENS, D), jnp.bfloat16),
        in_specs=[hbm, hbm, hbm, pl.BlockSpec(memory_space=pltpu.SMEM), hbm],
        out_specs=pl.BlockSpec(memory_space=pltpu.VMEM),
        scratch_shapes=[
            pltpu.VMEM((TOKENS, R), jnp.bfloat16),
            pltpu.VMEM((TOKENS, R), jnp.bfloat16),
            pltpu.VMEM((TOKENS, R), jnp.bfloat16),
            pltpu.VMEM((ROWS_W, D), jnp.bfloat16),
            pltpu.VMEM((HEADS, 2, 5, 3, 4, 16, HEAD_DIM), jnp.bfloat16),
            pltpu.VMEM((NA, NA, ROWS_W, D), jnp.bfloat16),
            pltpu.VMEM((TOKENS, 960), jnp.int32),
            pltpu.VMEM((TOKENS, R), jnp.bfloat16),
            pltpu.SemaphoreType.DMA((COPIES,)),
            pltpu.SemaphoreType.DMA((COPIES,)),
            pltpu.SemaphoreType.DMA((5,)),
        ],
        compiler_params=pltpu.CompilerParams(
            collective_id=0, has_side_effects=True, vmem_limit_bytes=67043328
        ),
    )(
        queries.reshape(TOKENS, R),
        keys.reshape(TOKENS, R),
        values.reshape(TOKENS, R),
        radius.T,
        out_weight,
    )
    return out.reshape(*shape, D)


def solution(mesh):
    return jax.shard_map(
        shards,
        mesh=mesh,
        in_specs=(
            P("ta", "ha", "wa", None),
            P("ta", "ha", "wa", None),
            P("ta", "ha", "wa", None),
            P(),
            P(("ha", "wa"), None),
        ),
        out_specs=P("ta", "ha", "wa", None),
        check_vma=False,
    )
```

time: 103 us -> 73 us (0.71)
  Pallas kernels: 96.9 us -> 70.9 us
  local copies, waits for them, and re-layouts: 5.39 us -> 1.92 us
    pallas_call x1, Pallas kernels: 96.9 us -> 70.9 us  [shards(): pl.pallas_call(kernel, out_shape=jax.ShapeDtypeStruct((TOKENS, D), jnp.bf...]
    unnamed x12 -> x1, local copies, waits for them, and re-layouts: 5.39 us -> 1.92 us
where the time goes in v2:
time: 73 us; the launch traced here: 72.8 us
  Pallas kernels  70.9 us (97%)
  local copies, waits for them, and re-layouts  1.92 us (3%)
    pallas_call x1, Pallas kernels, shards(): pl.pallas_call(kernel, out_shape=jax.ShapeDtypeStruct((TOKENS, D), jnp.bf...  70.9 us
    unnamed x1, local copies, waits for them, and re-layouts  1.92 us

profile of v2, /device:TPU:1, one launch (start us, length us, event | category | flops | bytes accessed | tf_op | source)
XLA Modules:
  0.0 72.8 jit_solution(4644723723825175627)
XLA Ops:
  0.0 70.9 %shard_map.55 = bf16[96,3072]{1,0:T(8,128)(2,1)} custom-call(bf16[96,1536]{1,0:T(8,128)(2,1)} %bitcast.6, bf16[96,1536]{1,0:T(8,128)(2,1)} %bitcast.7, bf16[96,1536]{1,0:T(8,128)(2,1)} %bitcast.8, s32[3,12]{1,0:T(4,128)} %bitcast.9, bf16[24,3072]{1,0:T(8,128)(2,1)} %w_hbm.1), custom_call_target="tpu_custom_call" | custom-call | tf_op jit(solution)/shard_map/pallas_call | solution.py:278
  70.9 1.9 %copy.7 = bf16[3,4,8,3072]{3,2,1,0:T(8,128)(2,1)} copy(bf16[3,4,8,3072]{3,2,1,0:T(8,128)(2,1)} %bitcast.5) | data formatting | bytes 1179648

commit v3 on v2

--- a/solution.py
+++ b/solution.py
@@ -12,7 +12,8 @@
 HEADS = 12
 HEAD_DIM = 128
 R = HEADS * HEAD_DIM
-CHUNKS = ((0, 4), (4, 3), (7, 3), (10, 2))
+CHUNKS = ((0, 3), (3, 4), (7, 3), (10, 2))
+OVER_WA = 2
 NA = 8
 FRAMES_HERE = 3
 TOKENS = 96
@@ -20,7 +21,7 @@
 HALF = D // 2
 PIECE = D // 4
 COLS = 512
-COPIES = 96
+COPIES = 136
 MESH = pl.DeviceIdType.MESH
 
 
@@ -77,7 +78,7 @@
 
     pl.semaphore_wait(barrier, len(greet))
 
-    started = []
+    started, shared = [], []
 
     def send(src, dst, who):
         i = len(started)
@@ -101,16 +102,16 @@
     ha_up, ha_down = {"ha": step(ha, 1)}, {"ha": step(ha, -1)}
     wa_up, wa_down = {"wa": step(wa, 1)}, {"wa": step(wa, -1)}
 
-    y_copies = []
+    own = pltpu.make_async_copy(w_ref.at[:, mine], wbuf.at[ha, wa, :, mine], local_sems.at[4])
+    own.start()
+
+    cols = piece(par, 1 - core)
+    y_copies = [send(w_ref.at[:, cols], wbuf.at[ha, wa, :, cols], other_core)]
     for where in ({"ta": twin, "ha": 1}, {"ta": ta, "ha": 1}, {"ta": twin, "ha": 2}):
         for e in (0, 1):
             there = {"ta": where["ta"], "ha": chip_at(where["ha"] * away, e)}
             cols = piece(par, lax.rem(core + e, 2))
             y_copies.append(send(w_ref.at[:, cols], wbuf.at[ha, wa, :, cols], there))
-    cols = piece(par, 1 - core)
-    y_copies.append(send(w_ref.at[:, cols], wbuf.at[ha, wa, :, cols], other_core))
-    own = pltpu.make_async_copy(w_ref.at[:, mine], wbuf.at[ha, wa, :, mine], local_sems.at[4])
-    own.start()
 
     def rim(frames):
         return [
@@ -124,29 +125,100 @@
             send(kv.at[:, :, frames, 1, 3], kv.at[:, :, frames, outer, 3], other_core),
         ]
 
-    def rows(c, frames):
-        first, count = CHUNKS[c]
-        src = kv.at[pl.ds(first, count), :, frames, 1, 1:3]
-        return [
-            send(src, kv.at[pl.ds(first, count), :, frames, 0, 1:3], ha_up),
-            send(src, kv.at[pl.ds(first, count), :, frames, 2, 1:3], ha_down),
+    facing = 2 - outer
+    beyond = step(ha, outer - 1)
+    three, two, twin_two = pl.ds(2 * odd, 3), pl.ds(3 - 3 * odd, 2), pl.ds(3 * odd, 2)
+
+    def heads_of(c):
+        return pl.ds(CHUNKS[c][0], CHUNKS[c][1])
+
+    def rows_inside(c, frames):
+        heads = heads_of(c)
+        return [send(kv.at[heads, :, frames, 1, 1:3], kv.at[heads, :, frames, outer, 1:3], other_core)]
+
+    def rows_outside(c, frames):
+        heads = heads_of(c)
+        return [send(kv.at[heads, :, frames, 1, 1:3], kv.at[heads, :, frames, facing, 1:3], {"ha": beyond})]
+
+    def rows_shared(c, cols):
+        heads = heads_of(c)
+        copies = [send(kv.at[heads, :, three, 1, cols], kv.at[heads, :, three, facing, cols], {"ha": beyond})]
+        i = len(started)
+        both = [
+            pltpu.make_async_remote_copy(
+                src_ref=kv.at[heads, :, two, 1, cols], dst_ref=kv.at[heads, :, at, facing, cols],
+                send_sem=send_sems.at[i + k], recv_sem=recv_sems.at[i],
+                device_id=where, device_id_type=MESH,
+            )
+            for k, (at, where) in enumerate(
+                ((twin_two, {"ta": twin, "ha": beyond}), (two, {"ta": ta, "ha": beyond}))
+            )
         ]
+
+        @pl.when(odd == core)
+        def _():
+            for copy in both:
+                copy.start()
+
+        started.extend([None, None])
+        shared.extend(both)
+        return copies + [both[1]]
 
     def outer_rim(c):
         arrived(h_copies[c])
-        heads = pl.ds(CHUNKS[c][0], CHUNKS[c][1])
+        heads = heads_of(c)
         return [
             send(kv.at[heads, :, :, outer, 2], kv.at[heads, :, :, outer, 0], wa_up),
             send(kv.at[heads, :, :, outer, 1], kv.at[heads, :, :, outer, 3], wa_down),
         ]
 
-    OWN = slice(1, 4)
-    w_own = rim(OWN)
+    OWN, ALL = slice(1, 4), slice(0, 5)
     t_copies = [
         send(kv.at[:, :, 3, 1, 1:3], kv.at[:, :, 0, 1, 1:3], ta_up),
         send(kv.at[:, :, 1, 1, 1:3], kv.at[:, :, 4, 1, 1:3], ta_down),
     ]
-    h_copies = [rows(0, OWN)]
+    h_copies = [rows_outside(0, OWN) + rows_inside(0, OWN)]
+
+    x_copies, pair_copies, rings = {}, [], {}
+    UNITS = (0, 1, 2, 3)
+
+    def unit(u, at, cols):
+        chip = lax.rem(lax.div(ha, 2) + (0, away, -away, 2)[u] + NA, NA // 2)
+        return wbuf.at[pl.ds(2 * chip, 2), at, :, cols]
+
+    def ring(u, way, r):
+        at = step(wa, way * (1 - r))
+        return send(unit(u, at, mine), unit(u, at, mine), wa_up if way == 1 else wa_down)
+
+    def across_x(u, at, key):
+        x_copies[key, u] = at, send(unit(u, at, mine), unit(u, at, mine), {"ta": step(ta, 2 if u % 2 else -2)})
+
+    def to_partner(key):
+        for u in UNITS:
+            at, copy = x_copies[key, u]
+            copy.wait_recv()
+            cols = pl.ds(pl.multiple_of(core * HALF, 128), HALF)
+            pair_copies.append(send(unit(u, at, cols), unit(u, at, cols), other_core))
+
+    def first_ring(u):
+        arrived(y_copies[:1] if u == 0 else y_copies[2 * u - 1 : 2 * u + 1])
+        for way in (1, -1):
+            rings[u, way, 1] = ring(u, way, 1)
+        across_x(u, wa, 0)
+
+    def next_ring(r, units=UNITS):
+        for u in units:
+            for way in (1, -1):
+                if (u, way, r) not in rings:
+                    continue
+                rings[u, way, r].wait_recv()
+                if r < 3 or (r == 3 and way == (-1 if u // 2 else 1)):
+                    rings[u, way, r + 1] = ring(u, way, r + 1)
+                across_x(u, step(wa, -way * r), way * r if r < 4 else 4)
+
+    own.wait()
+    first_ring(0)
+    w_own = rim(OWN)
 
     qi = lax.broadcasted_iota(jnp.int32, (TOKENS, 960), 0)
     kj = lax.broadcasted_iota(jnp.int32, (TOKENS, 960), 1)
@@ -161,43 +233,8 @@
     kind = jnp.where(dt == 0, 0, 1) + jnp.where(dh == 0, 0, 2) + jnp.where(dw == 0, 0, 4)
     code[...] = kind + jnp.where(never, 8, 0)
 
-    x_copies, pair_copies = {}, []
-
-    def block(half, at, cols):
-        return wbuf.at[4 * half : 4 * half + 4, at, :, cols]
-
-    def ring(half, way, r):
-        at = step(wa, way * (1 - r))
-        return send(block(half, at, mine), block(half, at, mine), wa_up if way == 1 else wa_down)
-
-    def across_x(half, at, key):
-        x_copies[key, half] = at, send(
-            block(half, at, mine), block(half, at, mine), {"ta": step(ta, 2 if half else -2)}
-        )
-
-    def to_partner(key, half):
-        at, copy = x_copies[key, half]
-        copy.wait_recv()
-        cols = pl.ds(pl.multiple_of(core * HALF, 128), HALF)
-        pair_copies.append(send(block(half, at, cols), block(half, at, cols), other_core))
-
-    own.wait()
-    arrived(y_copies)
-    rings = {}
-    for half in (0, 1):
-        for way in (1, -1):
-            rings[half, way, 1] = ring(half, way, 1)
-        across_x(half, wa, 0)
-
-    def next_ring(r, halves=(0, 1)):
-        for half in halves:
-            for way in (1, -1):
-                if (half, way, r) not in rings:
-                    continue
-                rings[half, way, r].wait_recv()
-                if r < 3 or (r == 3 and way == 1 - 2 * half):
-                    rings[half, way, r + 1] = ring(half, way, r + 1)
-                across_x(half, step(wa, -way * r), way * r if r < 4 else 4)
+    for u in (1, 2, 3):
+        first_ring(u)
 
     def attend(c):
         arrived(o_copies[c])
@@ -220,41 +257,40 @@
             out = jnp.dot(probs, v, preferred_element_type=jnp.float32)
             att[:, lanes] = out.astype(jnp.bfloat16)
 
-    ALL = slice(0, 5)
     arrived(w_own)
     c_copies = rim_across(OWN)
     next_ring(1, (0,))
     arrived(t_copies)
-    h_copies[0] = h_copies[0] + rows(0, 0) + rows(0, 4)
-    h_copies += [rows(c, ALL) for c in range(1, len(CHUNKS))]
     w_t = [rim(0), rim(4)]
-    next_ring(1, (1,))
-    next_ring(2)
-    o_copies = [outer_rim(0)]
+    for f in (0, 4):
+        h_copies[0] = h_copies[0] + rows_outside(0, f) + rows_inside(0, f)
+    h_copies += [rows_shared(c, slice(1, 3)) for c in range(1, OVER_WA)]
+    for c in range(1, OVER_WA):
+        h_copies[c] = h_copies[c] + rows_inside(c, ALL)
+    next_ring(1, (1, 2, 3))
     for copies, f in zip(w_t, (0, 4)):
         arrived(copies)
         c_copies += rim_across(f)
-    to_partner(0, 0)
-    to_partner(0, 1)
-    next_ring(3, (0,))
-    o_copies.append(outer_rim(1))
-    next_ring(3, (1,))
+    for c in range(OVER_WA, len(CHUNKS)):
+        h_copies.append(rows_shared(c, slice(0, 4)) + rows_inside(c, ALL))
+    next_ring(2)
+    o_copies = [outer_rim(0)]
+    to_partner(0)
+    next_ring(3, (0, 1))
+    o_copies += [outer_rim(c) for c in range(1, OVER_WA)]
+    o_copies += h_copies[OVER_WA:]
+    next_ring(3, (2, 3))
     loads[3].wait()
     arrived(c_copies)
-    o_copies.append(outer_rim(2))
     for key in (1, -1):
-        to_partner(key, 0)
-        to_partner(key, 1)
+        to_partner(key)
     next_ring(4)
-    o_copies.append(outer_rim(3))
     attend(0)
     for key in (2, -2):
-        to_partner(key, 0)
-        to_partner(key, 1)
+        to_partner(key)
     attend(1)
     for key in (3, -3, 4):
-        to_partner(key, 0)
-        to_partner(key, 1)
+        to_partner(key)
     attend(2)
     attend(3)
 
@@ -269,7 +305,13 @@
     arrived(pair_copies)
     project(1 - core)
     for copy in started:
-        copy.wait_send()
+        if copy is not None:
+            copy.wait_send()
+
+    @pl.when(odd == core)
+    def _():
+        for copy in shared:
+            copy.wait_send()
 
 
 def shards(queries, keys, values, radius, out_weight):

time: 73 us -> 70.5 us (0.966)
  Pallas kernels: 70.9 us -> 68.4 us
    pallas_call x1, Pallas kernels: 70.9 us -> 68.4 us  [shards(): pl.pallas_call(kernel, out_shape=jax.ShapeDtypeStruct((TOKENS, D), jnp.bf...]
where the time goes in v3:
time: 70.5 us; the launch traced here: 70.3 us
  Pallas kernels  68.4 us (97%)
  local copies, waits for them, and re-layouts  1.92 us (3%)
    pallas_call x1, Pallas kernels, shards(): pl.pallas_call(kernel, out_shape=jax.ShapeDtypeStruct((TOKENS, D), jnp.bf...  68.4 us
    unnamed x1, local copies, waits for them, and re-layouts  1.92 us

profile of v3, /device:TPU:1, one launch (start us, length us, event | category | flops | bytes accessed | tf_op | source)
XLA Modules:
  0.0 70.3 jit_solution(15782830345692121594)
XLA Ops:
  0.0 68.4 %shard_map.55 = bf16[96,3072]{1,0:T(8,128)(2,1)} custom-call(bf16[96,1536]{1,0:T(8,128)(2,1)} %bitcast.6, bf16[96,1536]{1,0:T(8,128)(2,1)} %bitcast.7, bf16[96,1536]{1,0:T(8,128)(2,1)} %bitcast.8, s32[3,12]{1,0:T(4,128)} %bitcast.9, bf16[24,3072]{1,0:T(8,128)(2,1)} %w_hbm.1), custom_call_target="tpu_custom_call" | custom-call | tf_op jit(solution)/shard_map/pallas_call | solution.py:320
  68.4 1.9 %copy.7 = bf16[3,4,8,3072]{3,2,1,0:T(8,128)(2,1)} copy(bf16[3,4,8,3072]{3,2,1,0:T(8,128)(2,1)} %bitcast.5) | data formatting | bytes 1179648
